TPU v7x, 256 devices: a whole 4x4x8 slice. The times are simulated.
256 devices in a mesh: tm: 32 (over y, z), eval: 8 (over x, core).
Axes of the slice: x: 4, y: 4, z: 8, core: 2. Of those that a mesh axis runs over, the one named last changes fastest.
Arguments:
- hidden: bfloat16 [512, 1024, 1536], P('tm', 'eval'), may hold values from -9 to 9
- modulation: float32 [512, 2, 1536], P('tm'), may hold values from -2 to 3
- head_weight: bfloat16 [64, 1536], replicated, may hold values from -1 to 1
- real_score: bfloat16 [64, 21, 16, 4096], P('eval', None, None, 'tm'), may hold values from -152917 to 152917
- fake_score: bfloat16 [64, 21, 16, 4096], P('eval', None, None, 'tm'), may hold values from -152917 to 152917
- window_start: int32 [64], P('eval'), may hold values from 0 to 491, as said below
- timestep: int32 [64], P('eval'), may hold values from 20 to 999
Outputs:
- d_hidden: bfloat16 [512, 1024, 1536], P('tm', 'eval')
- head_grad: float32 [64, 1536], replicated
- mod_grad: float32 [512, 2, 1536], P('tm')
Inputs may be any that keep to these rules, and one draw needn't show every extreme that they name: `window_start`: every window lies inside the rollout; one window starts at frame 0 and one at the last possible frame.
All inputs are finite; a program needn't handle non-finite values.
Results may differ from a plain program's by a relative error of at most 0.0012.
The roundings to bfloat16 on the way count: a program that leaves them out, or rounds other values in their place, can miss the bound.
Values may be sent and summed in bfloat16 or wider, within the bound.
No kernel may reach another device: no remote copies, remote signals or barrier semaphores. Data moves between devices by JAX's collectives and lax.ppermute only.
A program may use at most 128 MiB of HBM per device.

v0:
```python
import jax
import jax.numpy as jnp
from jax import lax
from jax.sharding import PartitionSpec as P

C = 16
PATCH = 4
WIN = 21
TOK = 1024


def layer_norm(values_in):
    values = values_in.astype(jnp.float32)
    center = jnp.mean(values, axis=-1, keepdims=True)
    shifted = values - center
    inv_std = lax.rsqrt(jnp.mean(shifted * shifted, axis=-1, keepdims=True) + 1e-06)
    return (shifted * inv_std, inv_std)


def per_device(hidden, modulation, head_weight, real_score, fake_score, window_start, timestep):
    frames_dev, tok_dev, width = hidden.shape
    shift = modulation[:, 0][:, None, :]
    scale = modulation[:, 1][:, None, :]
    normed, inv_std = layer_norm(hidden)
    adapted = (normed * (1.0 + scale) + shift).astype(jnp.bfloat16)
    head_out = jnp.einsum("ftd,od->fto", adapted, head_weight, preferred_element_type=jnp.float32)
    latent = head_out.astype(jnp.bfloat16).reshape(frames_dev, tok_dev, C, PATCH)
    latent = latent.transpose(0, 2, 1, 3).reshape(frames_dev, C, tok_dev * PATCH)
    frame_whole = lax.all_gather(latent, "eval", axis=2, tiled=True)
    latent_all = lax.all_to_all(frame_whole, "tm", split_axis=2, concat_axis=0, tiled=True)
    pixel_block = latent_all.shape[2]
    frame_index = window_start[:, None] + jnp.arange(WIN, dtype=jnp.int32)[None, :]
    window_latent = latent_all[frame_index].astype(jnp.float32)
    real_values = real_score.astype(jnp.float32)
    fake_values = fake_score.astype(jnp.float32)
    abs_sums = jnp.sum(jnp.abs(window_latent - real_values), axis=(1, 2, 3))
    totals = lax.psum(abs_sums, "tm")
    normalizer = totals / (WIN * C * PATCH * TOK) + 1e-05
    weight = timestep.astype(jnp.float32) / 1000.0 / normalizer
    window_grad = weight[:, None, None, None] * (fake_values - real_values)
    group_grad = (
        jnp.zeros(latent_all.shape, jnp.float32)
        .at[frame_index.reshape(-1)]
        .add(window_grad.reshape(-1, C, pixel_block))
    )
    home = lax.all_to_all(group_grad, "tm", split_axis=0, concat_axis=2, tiled=True)
    owner_grad = lax.psum_scatter(home, "eval", scatter_dimension=2, tiled=True)
    upstream = owner_grad.reshape(frames_dev, C, tok_dev, PATCH).transpose(0, 2, 1, 3)
    upstream = upstream.reshape(frames_dev, tok_dev, C * PATCH).astype(jnp.bfloat16)
    d_adapted = jnp.einsum("fto,od->ftd", upstream, head_weight, preferred_element_type=jnp.float32)
    head_part = jnp.einsum("fto,ftd->od", upstream, adapted, preferred_element_type=jnp.float32)
    mod_part = jnp.stack([jnp.sum(d_adapted, axis=1), jnp.sum(d_adapted * normed, axis=1)], axis=1)
    head_grad = lax.psum(head_part, ("tm", "eval"))
    mod_grad = lax.psum(mod_part, "eval")
    d_normed = d_adapted * (1.0 + scale)
    d_hidden = inv_std * (
        d_normed
        - jnp.mean(d_normed, axis=-1, keepdims=True)
        - normed * jnp.mean(d_normed * normed, axis=-1, keepdims=True)
    )
    return (d_hidden.astype(jnp.bfloat16), head_grad, mod_grad)


def solution(mesh):
    placed = (
        P("tm", "eval", None),
        P("tm", None, None),
        P(),
        P("eval", None, None, "tm"),
        P("eval", None, None, "tm"),
        P("eval"),
        P("eval"),
    )
    return jax.shard_map(
        per_device,
        mesh=mesh,
        in_specs=placed,
        out_specs=(P("tm", "eval", None), P(), P("tm", None, None)),
        check_vma=False,
    )
```

profile of v0, /device:TPU:1, one launch (start us, length us, event | category | flops | bytes accessed | tf_op | source)
XLA Modules:
  0.0 757.5 jit_solution(7772980234880290092)
XLA Ops:
  7.2 0.0 copy-start
  7.2 0.0 copy-start.3
  7.2 0.0 all-gather.2.cloned.1.call-start
  7.2 0.0 copy-start.1
  7.2 3.8 convert_reduce_fusion
  11.1 4.6 fusion.13
  15.7 0.0 copy-done.3
  15.7 0.2 fusion.33
  15.9 0.0 copy-done
  15.9 0.0 copy-done.1
  15.9 3.1 fusion.24
  19.0 3.2 copy.49
  22.2 2.3 copy.50
  24.5 0.0 all-gather.2.cloned.1.call-update
  24.5 32.2 %all-gather.2.cloned.1.call-done = bf16[16,16,4096]{2,1,0:T(8,128)(2,1)} async-done(((bf16[16,16,512]{2,1,0:T(8,128)(2,1)}), bf16[16,16,4096]{2,1,0:T(8,128)(2,1)}) %all-gather.2.cloned.1.call-update) | async-done | bytes 2097168 | tf_op jit(solution)/shard_map/all_gather | solution.py:29
  56.7 15.4 %copy.51 = bf16[16,16,4096]{1,0,2:T(8,128)(2,1)} copy(bf16[16,16,4096]{2,1,0:T(8,128)(2,1)} %all-gather.2.cloned.1.call-done) | data formatting | bytes 4194304 | tf_op jit(solution)/shard_map/all_gather | solution.py:29
  72.0 0.0 copy-start.4
  72.0 20.8 %reshape.132 = bf16[32,2,16384]{2,1,0:T(2,128)(2,1)} reshape(bf16[4096,16,16]{2,1,0:T(8,128)(2,1)} %bitcast.43) | data formatting | bytes 4194304
  92.8 9.6 %all-to-all-start = ((bf16[32,2,16384]{2,1,0:T(2,128)(2,1)}), bf16[32,2,16384]{2,1,0:T(2,128)(2,1)S(1)}, u32[]{:S(2)}, u32[]{:S(2)}) async-start(bf16[32,2,16384]{2,1,0:T(2,128)(2,1)} %reshape.132), calls=%async_computation | async-start | bytes 4194304 | tf_op jit(solution)/shard_map/all_to_all | solution.py:30
  102.4 0.0 reduce-scatter.2.cloned.1.call-start
  102.5 0.0 copy-done.4
  102.5 0.1 compare_select_fusion
  102.5 0.1 reshape.114
  102.6 0.1 iota_add_fusion
  102.7 0.1 add.106
  102.8 48.5 %all-to-all-done = bf16[32,2,16384]{2,1,0:T(2,128)(2,1)S(1)} async-done(((bf16[32,2,16384]{2,1,0:T(2,128)(2,1)}), bf16[32,2,16384]{2,1,0:T(2,128)(2,1)S(1)}, u32[]{:S(2)}, u32[]{:S(2)}) %all-to-all-start) | async-done | bytes 2097184 | tf_op jit(solution)/shard_map/all_to_all | solution.py:30
  151.3 14.4 %reshape.133 = bf16[4096,16,16]{2,1,0:T(8,128)(2,1)} reshape(bf16[32,2,16384]{2,1,0:T(2,128)(2,1)S(1)} %all-to-all-done) | data formatting | bytes 4194304
  165.7 0.0 copy-start.2
  165.7 0.0 copy-start.5
  165.7 14.4 %copy.53 = bf16[32,16,16,128]{3,2,1,0:T(8,128)(2,1)S(1)} copy(bf16[32,16,16,128]{2,1,3,0:T(8,128)(2,1)} %bitcast.44) | data formatting | bytes 4194304 | tf_op jit(solution)/shard_map/all_to_all | solution.py:30
  180.1 1.6 gather_fusion
  181.7 0.0 copy-done.2
  181.7 1.4 fusion.22
  183.1 60.2 %psum.21 = f32[8]{0:T(128)S(1)} all-reduce(f32[8]{0:T(128)S(1)} %fusion.22), channel_id=1, replica_groups=mesh['tm'=32,'eval'=8] {'tm'}, use_global_device_ids=true, to_apply=%region_3.0 | all-reduce | flops 8 | bytes 64 | tf_op jit(solution)/shard_map/psum | solution.py:37
  243.4 0.0 copy-done.5
  243.4 1.3 fusion.23
  244.7 2.3 broadcast_in_dim.2
  247.0 19.7 %scatter_fusion = f32[512,16,128]{2,1,0:T(8,128)} fusion(f32[512,16,128]{2,1,0:T(8,128)} %broadcast_in_dim.2, s32[168]{0:T(256)S(1)} %bitcast.59, f32[168,16,128]{2,1,0:T(8,128)S(1)} %bitcast.51), kind=kCustom, calls=%fused_computation.1 | custom fusion | flops 344064 | bytes 4129440 | tf_op jit(solution)/shard_map/scatter-add | solution.py:44
  266.7 83.4 %all_to_all.36 = f32[512,16,128]{2,1,0:T(8,128)S(1)} all-to-all(f32[512,16,128]{2,1,0:T(8,128)} %scatter_fusion), channel_id=1, replica_groups=mesh['tm'=32,'eval'=8] {'tm'}, dimensions={0} | all-to-all | bytes 8388608 | tf_op jit(solution)/shard_map/all_to_all | solution.py:46
  350.1 2.5 copy.76
  352.7 0.0 reduce-scatter.2.cloned.1.call-update
  352.7 0.0 all-reduce.5.cloned.1.call-start
  352.7 50.7 %reduce-scatter.2.cloned.1.call-done = f32[16,16,512]{2,1,0:T(8,128)} async-done(((f32[16,16,4096]{2,1,0:T(8,128)}), f32[16,16,512]{2,1,0:T(8,128)}) %reduce-scatter.2.cloned.1.call-update) | async-done | bytes 524304 | tf_op jit(solution)/shard_map/reduce_scatter | solution.py:47
  403.4 1.1 convert_element_type.43
  404.5 2.8 copy.55
  407.3 0.0 slice-start
  407.3 4.0 copy.56
  411.3 0.0 slice-start.1
  411.3 10.1 %fusion.12 = (f32[16,1536]{1,0:T(8,128)S(1)}, f32[16,128]{1,0:T(8,128)S(1)}, f32[16,128]{1,0:T(8,128)S(1)}, f32[16,1536]{1,0:T(8,128)S(1)}, f32[16,128,1536]{2,1,0:T(8,128)}) fusion(bf16[16,128,1536]{2,1,0:T(8,128)(2,1)} %param.7, f32[16,128]{1,0:T(8,128)S(1)} %add_rsqrt_fusion, f32[16,128]{1,0:T(8,128)S(1)} %broadcast_multiply_fusion.2, ...), kind=kOutput, calls=%fused_computation.16 | convolution fusion | flops 434057216 | bytes 19660800 | tf_op jit(solution)/shard_map/fto,od->ftd/dot_general | solution.py:50
  421.4 0.0 slice-done
  421.4 0.0 slice-done.1
  421.4 3.5 fusion.18
  424.9 0.7 pad_maximum_fusion
  425.6 0.0 all-reduce.5.cloned.1.call-update
  425.6 0.0 all-reduce.3.cloned.1.call-start
  425.7 0.5 all-reduce.3.cloned.1.call-update
  426.2 10.5 %fusion.11 = bf16[16,128,1536]{2,1,0:T(8,128)(2,1)} fusion(bf16[16,128,1536]{2,1,0:T(8,128)(2,1)} %param.7, f32[16,128,1536]{2,1,0:T(8,128)} %get-tuple-element.24, f32[16,128]{1,0:T(8,128)S(1)} %broadcast_multiply_fusion, f32[16,128]{1,0:T(8,128)S(1)} %broadcast_multiply_fusion.1, f32[16,1536]{1,0:T(8,128)S(1)} %get-tuple-element.26, ...), kind=kLoop, calls=%fused_computation.15 | loop fusion | flops 28311552 | bytes 25296896 | tf_op jit(solution)/shard_map/convert_element_type | solution.py:61
  436.7 53.9 %all-reduce.5.cloned.1.call-done = f32[16,2,1536]{2,0,1:T(8,128)} async-done(((f32[16,2,1536]{2,0,1:T(8,128)}), f32[16,2,1536]{2,0,1:T(8,128)}) %all-reduce.5.cloned.1.call-update) | async-done | bytes 196624 | tf_op jit(solution)/shard_map/psum | solution.py:54
  490.5 1.8 copy.59
  492.3 256.9 %all-reduce.3.cloned.1.call-done = f32[64,1536]{1,0:T(8,128)} async-done(((f32[64,1536]{1,0:T(8,128)}), f32[64,1536]{1,0:T(8,128)}) %all-reduce.3.cloned.1.call-update) | async-done | bytes 393232 | tf_op jit(solution)/shard_map/psum | solution.py:53
  749.2 1.8 copy.80
  (9 shorter events, 0.1 us)
Async XLA Ops:
  7.2 8.7 %copy-start = (bf16[64,1536]{1,0:T(8,128)(2,1)S(1)}, bf16[64,1536]{1,0:T(8,128)(2,1)}, u32[]{:S(2)}) copy-start(bf16[64,1536]{1,0:T(8,128)(2,1)} %param.9) | copy-start | bytes 589828
  7.2 8.5 %copy-start.3 = (f32[16,2,1536]{2,1,0:T(2,128)S(1)}, f32[16,2,1536]{2,1,0:T(2,128)}, u32[]{:S(2)}) copy-start(f32[16,2,1536]{2,1,0:T(2,128)} %param.8) | copy-start | bytes 589828
  7.2 49.5 %all-gather.2.cloned.1.call-start = ((), (), s32[]{:S(2)}) async-start(), calls=%async_computation.3 | async-start | bytes 2359296 | tf_op jit(solution)/shard_map/all_gather | solution.py:29
  7.2 8.7 %copy-start.1 = (bf16[16,128,1536]{2,1,0:T(8,128)(2,1)S(1)}, bf16[16,128,1536]{2,1,0:T(8,128)(2,1)}, u32[]{:S(2)}) copy-start(bf16[16,128,1536]{2,1,0:T(8,128)(2,1)} %param.7) | copy-start | bytes 18874372
  72.0 30.4 %copy-start.4 = (s32[8]{0:T(128)S(1)}, s32[8]{0:T(128)}, u32[]{:S(2)}) copy-start(s32[8]{0:T(128)} %param.12) | copy-start | bytes 100
  92.8 58.5 %all-to-all-start = ((bf16[32,2,16384]{2,1,0:T(2,128)(2,1)}), bf16[32,2,16384]{2,1,0:T(2,128)(2,1)S(1)}, u32[]{:S(2)}, u32[]{:S(2)}) async-start(bf16[32,2,16384]{2,1,0:T(2,128)(2,1)} %reshape.132), calls=%async_computation | async-start | bytes 4194304 | tf_op jit(solution)/shard_map/all_to_all | solution.py:30
  102.4 301.0 %reduce-scatter.2.cloned.1.call-start = ((), (), s32[]{:S(2)}) async-start(), calls=%async_computation.4 | async-start | bytes 4718592 | tf_op jit(solution)/shard_map/reduce_scatter | solution.py:47
  165.7 16.0 %copy-start.2 = (bf16[8,21,16,128]{3,2,1,0:T(8,128)(2,1)S(1)}, bf16[8,21,16,128]{3,2,1,0:T(8,128)(2,1)}, u32[]{:S(2)}) copy-start(bf16[8,21,16,128]{3,2,1,0:T(8,128)(2,1)} %param.10) | copy-start | bytes 2064388
  165.7 77.7 %copy-start.5 = (s32[8]{0:T(128)S(1)}, s32[8]{0:T(128)}, u32[]{:S(2)}) copy-start(s32[8]{0:T(128)} %param.13) | copy-start | bytes 100
  352.7 137.9 %all-reduce.5.cloned.1.call-start = ((), (), s32[]{:S(2)}) async-start(), calls=%async_computation.6 | async-start | bytes 393216 | tf_op jit(solution)/shard_map/psum | solution.py:54
  407.3 14.2 %slice-start = ((s8[6291456]{0:T(1024)(128)(4,1)}), s8[2097152]{0:T(1024)(128)(4,1)S(1)}, s32[]{:S(2)}) async-start(s8[6291456]{0:T(1024)(128)(4,1)} %bitcast.45), calls=%async_computation.7 | async-start | bytes 4194304
  411.3 10.1 %slice-start.1 = ((s8[6291456]{0:T(1024)(128)(4,1)}), s8[4194304]{0:T(1024)(128)(4,1)S(1)}, s32[]{:S(2)}) async-start(s8[6291456]{0:T(1024)(128)(4,1)} %bitcast.45), calls=%async_computation.8 | async-start | bytes 8388608
  425.6 323.6 %all-reduce.3.cloned.1.call-start = ((), (), s32[]{:S(2)}) async-start(), calls=%async_computation.5 | async-start | bytes 786432 | tf_op jit(solution)/shard_map/psum | solution.py:53
Sparse Core Ops, SparseCore 0:
  24.6 31.9 all-gather.1
  352.8 50.5 reduce-scatter.1
  425.7 64.7 all-reduce.4
  496.5 252.6 all-reduce.2
where the time goes:
time: 760 us; the launch traced here: 758 us
  waiting for transfers between devices  443 us (58%)
  blocking collectives  144 us (19%)
  local copies, waits for them, and re-layouts  87.5 us (12%)
  other arithmetic  43.3 us (6%)
  matrix products  16.6 us (2%)
  between operations  14 us (2%)
  starting transfers between devices  9.73 us (1%)
    psum x1, waiting for transfers between devices, per_device(): head_grad = lax.psum(head_part, ('tm', 'eval'))  257 us
    all_to_all x1, blocking collectives, per_device(): lax.all_to_all(group_grad, 'tm', split_axis=0, concat_axis=2, tiled=True)  83.4 us
    psum x1, blocking collectives, per_device(): totals = lax.psum(abs_sums, 'tm')  60.2 us
    psum x1, waiting for transfers between devices, per_device(): mod_grad = lax.psum(mod_part, 'eval')  53.9 us
    reduce_scatter x1, waiting for transfers between devices, per_device(): owner_grad = lax.psum_scatter(home, 'eval', scatter_dimension=2, tiled=True)  50.7 us
    all_to_all x1, waiting for transfers between devices, per_device(): lax.all_to_all(frame_whole, 'tm', split_axis=2, concat_axis=0, tiled=True)  48.5 us
    unnamed x20, local copies, waits for them, and re-layouts  38.7 us
    all_gather x1, waiting for transfers between devices, per_device(): frame_whole = lax.all_gather(latent, 'eval', axis=2, tiled=True)  32.2 us
  transfers between devices with their start and end apart: 5, of which 5 were waited for; matrix products, arithmetic and copies ran while one was open for 2% of the time, Pallas kernels for 0%

commit v1 on v0

--- a/solution.py
+++ b/solution.py
@@ -50,7 +50,7 @@
     d_adapted = jnp.einsum("fto,od->ftd", upstream, head_weight, preferred_element_type=jnp.float32)
     head_part = jnp.einsum("fto,ftd->od", upstream, adapted, preferred_element_type=jnp.float32)
     mod_part = jnp.stack([jnp.sum(d_adapted, axis=1), jnp.sum(d_adapted * normed, axis=1)], axis=1)
-    head_grad = lax.psum(head_part, ("tm", "eval"))
+    head_grad = lax.psum(lax.psum(head_part, "tm"), "eval")
     mod_grad = lax.psum(mod_part, "eval")
     d_normed = d_adapted * (1.0 + scale)
     d_hidden = inv_std * (

time: 760 us -> 652 us (0.86)
  waiting for transfers between devices: 443 us -> 334 us
    psum x2, waiting for transfers between devices: 311 us -> 202 us  [per_device(): head_grad = lax.psum(lax.psum(head_part, 'tm'), 'eval')]
where the time goes in v1:
time: 652 us; the launch traced here: 648 us
  waiting for transfers between devices  334 us (51%)
  blocking collectives  144 us (22%)
  local copies, waits for them, and re-layouts  87.5 us (13%)
  other arithmetic  43.3 us (7%)
  matrix products  16.6 us (3%)
  between operations  14 us (2%)
  starting transfers between devices  9.73 us (1%)
    psum x2, waiting for transfers between devices, per_device(): head_grad = lax.psum(lax.psum(head_part, 'tm'), 'eval')  202 us
    all_to_all x1, blocking collectives, per_device(): lax.all_to_all(group_grad, 'tm', split_axis=0, concat_axis=2, tiled=True)  83.4 us
    psum x1, blocking collectives, per_device(): totals = lax.psum(abs_sums, 'tm')  60.2 us
    reduce_scatter x1, waiting for transfers between devices, per_device(): owner_grad = lax.psum_scatter(home, 'eval', scatter_dimension=2, tiled=True)  50.7 us
    all_to_all x1, waiting for transfers between devices, per_device(): lax.all_to_all(frame_whole, 'tm', split_axis=2, concat_axis=0, tiled=True)  48.5 us
    unnamed x20, local copies, waits for them, and re-layouts  38.7 us
    all_gather x1, waiting for transfers between devices, per_device(): frame_whole = lax.all_gather(latent, 'eval', axis=2, tiled=True)  32.2 us
    scatter-add x1, other arithmetic, per_device(): group_grad = jnp.zeros(latent_all.shape, jnp.float32).at[frame_index.resh...  19.7 us
  transfers between devices with their start and end apart: 5, of which 5 were waited for; matrix products, arithmetic and copies ran while one was open for 2% of the time, Pallas kernels for 0%

profile of v1, /device:TPU:1, one launch (start us, length us, event | category | flops | bytes accessed | tf_op | source)
XLA Modules:
  0.0 648.4 jit_solution(8560909026480814417)
XLA Ops:
  7.2 0.0 copy-start
  7.2 0.0 copy-start.3
  7.2 0.0 all-gather.2.cloned.1.call-start
  7.2 0.0 copy-start.1
  7.2 3.8 convert_reduce_fusion
  11.1 4.6 fusion.13
  15.7 0.0 copy-done.3
  15.7 0.2 fusion.33
  15.9 0.0 copy-done
  15.9 0.0 copy-done.1
  15.9 3.1 fusion.24
  19.0 3.2 copy.49
  22.2 2.3 copy.50
  24.5 0.0 all-gather.2.cloned.1.call-update
  24.5 32.2 %all-gather.2.cloned.1.call-done = bf16[16,16,4096]{2,1,0:T(8,128)(2,1)} async-done(((bf16[16,16,512]{2,1,0:T(8,128)(2,1)}), bf16[16,16,4096]{2,1,0:T(8,128)(2,1)}) %all-gather.2.cloned.1.call-update) | async-done | bytes 2097168 | tf_op jit(solution)/shard_map/all_gather | solution.py:29
  56.7 15.4 %copy.51 = bf16[16,16,4096]{1,0,2:T(8,128)(2,1)} copy(bf16[16,16,4096]{2,1,0:T(8,128)(2,1)} %all-gather.2.cloned.1.call-done) | data formatting | bytes 4194304 | tf_op jit(solution)/shard_map/all_gather | solution.py:29
  72.0 0.0 copy-start.4
  72.0 20.8 %reshape.132 = bf16[32,2,16384]{2,1,0:T(2,128)(2,1)} reshape(bf16[4096,16,16]{2,1,0:T(8,128)(2,1)} %bitcast.43) | data formatting | bytes 4194304
  92.8 9.6 %all-to-all-start = ((bf16[32,2,16384]{2,1,0:T(2,128)(2,1)}), bf16[32,2,16384]{2,1,0:T(2,128)(2,1)S(1)}, u32[]{:S(2)}, u32[]{:S(2)}) async-start(bf16[32,2,16384]{2,1,0:T(2,128)(2,1)} %reshape.132), calls=%async_computation | async-start | bytes 4194304 | tf_op jit(solution)/shard_map/all_to_all | solution.py:30
  102.4 0.0 reduce-scatter.2.cloned.1.call-start
  102.5 0.0 copy-done.4
  102.5 0.1 compare_select_fusion
  102.5 0.1 reshape.114
  102.6 0.1 iota_add_fusion
  102.7 0.1 add.108
  102.8 48.5 %all-to-all-done = bf16[32,2,16384]{2,1,0:T(2,128)(2,1)S(1)} async-done(((bf16[32,2,16384]{2,1,0:T(2,128)(2,1)}), bf16[32,2,16384]{2,1,0:T(2,128)(2,1)S(1)}, u32[]{:S(2)}, u32[]{:S(2)}) %all-to-all-start) | async-done | bytes 2097184 | tf_op jit(solution)/shard_map/all_to_all | solution.py:30
  151.3 14.4 %reshape.133 = bf16[4096,16,16]{2,1,0:T(8,128)(2,1)} reshape(bf16[32,2,16384]{2,1,0:T(2,128)(2,1)S(1)} %all-to-all-done) | data formatting | bytes 4194304
  165.7 0.0 copy-start.2
  165.7 0.0 copy-start.5
  165.7 14.4 %copy.53 = bf16[32,16,16,128]{3,2,1,0:T(8,128)(2,1)S(1)} copy(bf16[32,16,16,128]{2,1,3,0:T(8,128)(2,1)} %bitcast.44) | data formatting | bytes 4194304 | tf_op jit(solution)/shard_map/all_to_all | solution.py:30
  180.1 1.6 gather_fusion
  181.7 0.0 copy-done.2
  181.7 1.4 fusion.22
  183.1 60.2 %psum.28 = f32[8]{0:T(128)S(1)} all-reduce(f32[8]{0:T(128)S(1)} %fusion.22), channel_id=1, replica_groups=mesh['tm'=32,'eval'=8] {'tm'}, use_global_device_ids=true, to_apply=%region_3.0 | all-reduce | flops 8 | bytes 64 | tf_op jit(solution)/shard_map/psum | solution.py:37
  243.4 0.0 copy-done.5
  243.4 1.3 fusion.23
  244.7 2.3 broadcast_in_dim.2
  247.0 19.7 %scatter_fusion = f32[512,16,128]{2,1,0:T(8,128)} fusion(f32[512,16,128]{2,1,0:T(8,128)} %broadcast_in_dim.2, s32[168]{0:T(256)S(1)} %bitcast.59, f32[168,16,128]{2,1,0:T(8,128)S(1)} %bitcast.51), kind=kCustom, calls=%fused_computation.1 | custom fusion | flops 344064 | bytes 4129440 | tf_op jit(solution)/shard_map/scatter-add | solution.py:44
  266.7 83.4 %all_to_all.36 = f32[512,16,128]{2,1,0:T(8,128)S(1)} all-to-all(f32[512,16,128]{2,1,0:T(8,128)} %scatter_fusion), channel_id=1, replica_groups=mesh['tm'=32,'eval'=8] {'tm'}, dimensions={0} | all-to-all | bytes 8388608 | tf_op jit(solution)/shard_map/all_to_all | solution.py:46
  350.1 2.5 copy.76
  352.7 0.0 reduce-scatter.2.cloned.1.call-update
  352.7 0.0 all-reduce.4.cloned.1.call-start
  352.7 50.7 %reduce-scatter.2.cloned.1.call-done = f32[16,16,512]{2,1,0:T(8,128)} async-done(((f32[16,16,4096]{2,1,0:T(8,128)}), f32[16,16,512]{2,1,0:T(8,128)}) %reduce-scatter.2.cloned.1.call-update) | async-done | bytes 524304 | tf_op jit(solution)/shard_map/reduce_scatter | solution.py:47
  403.4 1.1 convert_element_type.43
  404.5 2.8 copy.55
  407.3 0.0 slice-start
  407.3 4.0 copy.56
  411.3 0.0 slice-start.1
  411.3 10.1 %fusion.12 = (f32[16,1536]{1,0:T(8,128)S(1)}, f32[16,128]{1,0:T(8,128)S(1)}, f32[16,128]{1,0:T(8,128)S(1)}, f32[16,1536]{1,0:T(8,128)S(1)}, f32[16,128,1536]{2,1,0:T(8,128)}) fusion(bf16[16,128,1536]{2,1,0:T(8,128)(2,1)} %param.7, f32[16,128]{1,0:T(8,128)S(1)} %add_rsqrt_fusion, f32[16,128]{1,0:T(8,128)S(1)} %broadcast_multiply_fusion.2, ...), kind=kOutput, calls=%fused_computation.16 | convolution fusion | flops 434057216 | bytes 19660800 | tf_op jit(solution)/shard_map/fto,od->ftd/dot_general | solution.py:50
  421.4 0.0 slice-done
  421.4 0.0 slice-done.1
  421.4 3.5 fusion.18
  424.9 0.0 all-reduce.4.cloned.1.call-update
  424.9 0.0 all-reduce.6.cloned.1.call-start
  425.0 0.7 pad_maximum_fusion
  425.7 143.4 %all-reduce.4.cloned.1.call-done = f32[64,1536]{1,0:T(8,128)} async-done(((f32[64,1536]{1,0:T(8,128)}), f32[64,1536]{1,0:T(8,128)}) %all-reduce.4.cloned.1.call-update) | async-done | bytes 393232 | tf_op jit(solution)/shard_map/psum | solution.py:53
  569.1 0.0 all-reduce.6.cloned.1.call-update
  569.1 10.5 %fusion.11 = bf16[16,128,1536]{2,1,0:T(8,128)(2,1)} fusion(bf16[16,128,1536]{2,1,0:T(8,128)(2,1)} %param.7, f32[16,128,1536]{2,1,0:T(8,128)} %get-tuple-element.26, f32[16,128]{1,0:T(8,128)S(1)} %broadcast_multiply_fusion, f32[16,128]{1,0:T(8,128)S(1)} %broadcast_multiply_fusion.1, f32[16,1536]{1,0:T(8,128)S(1)} %get-tuple-element.28, ...), kind=kLoop, calls=%fused_computation.15 | loop fusion | flops 28311552 | bytes 25296896 | tf_op jit(solution)/shard_map/convert_element_type | solution.py:61
  579.6 58.7 %all-reduce.6.cloned.1.call-done = (f32[64,1536]{1,0:T(8,128)}, f32[16,2,1536]{2,0,1:T(8,128)}) async-done(((f32[64,1536]{1,0:T(8,128)}, f32[16,2,1536]{2,0,1:T(8,128)}), (f32[64,1536]{1,0:T(8,128)}, f32[16,2,1536]{2,0,1:T(8,128)})) %all-reduce.6.cloned.1.call-update) | async-done | bytes 589840 | tf_op jit(solution)/shard_map/psum | solution.py:53
  638.3 1.8 copy.59
  640.0 1.8 copy.81
  (9 shorter events, 0.1 us)
Async XLA Ops:
  7.2 8.7 %copy-start = (bf16[64,1536]{1,0:T(8,128)(2,1)S(1)}, bf16[64,1536]{1,0:T(8,128)(2,1)}, u32[]{:S(2)}) copy-start(bf16[64,1536]{1,0:T(8,128)(2,1)} %param.9) | copy-start | bytes 589828
  7.2 8.5 %copy-start.3 = (f32[16,2,1536]{2,1,0:T(2,128)S(1)}, f32[16,2,1536]{2,1,0:T(2,128)}, u32[]{:S(2)}) copy-start(f32[16,2,1536]{2,1,0:T(2,128)} %param.8) | copy-start | bytes 589828
  7.2 49.5 %all-gather.2.cloned.1.call-start = ((), (), s32[]{:S(2)}) async-start(), calls=%async_computation.3 | async-start | bytes 2359296 | tf_op jit(solution)/shard_map/all_gather | solution.py:29
  7.2 8.7 %copy-start.1 = (bf16[16,128,1536]{2,1,0:T(8,128)(2,1)S(1)}, bf16[16,128,1536]{2,1,0:T(8,128)(2,1)}, u32[]{:S(2)}) copy-start(bf16[16,128,1536]{2,1,0:T(8,128)(2,1)} %param.7) | copy-start | bytes 18874372
  72.0 30.4 %copy-start.4 = (s32[8]{0:T(128)S(1)}, s32[8]{0:T(128)}, u32[]{:S(2)}) copy-start(s32[8]{0:T(128)} %param.12) | copy-start | bytes 100
  92.8 58.5 %all-to-all-start = ((bf16[32,2,16384]{2,1,0:T(2,128)(2,1)}), bf16[32,2,16384]{2,1,0:T(2,128)(2,1)S(1)}, u32[]{:S(2)}, u32[]{:S(2)}) async-start(bf16[32,2,16384]{2,1,0:T(2,128)(2,1)} %reshape.132), calls=%async_computation | async-start | bytes 4194304 | tf_op jit(solution)/shard_map/all_to_all | solution.py:30
  102.4 301.0 %reduce-scatter.2.cloned.1.call-start = ((), (), s32[]{:S(2)}) async-start(), calls=%async_computation.4 | async-start | bytes 4718592 | tf_op jit(solution)/shard_map/reduce_scatter | solution.py:47
  165.7 16.0 %copy-start.2 = (bf16[8,21,16,128]{3,2,1,0:T(8,128)(2,1)S(1)}, bf16[8,21,16,128]{3,2,1,0:T(8,128)(2,1)}, u32[]{:S(2)}) copy-start(bf16[8,21,16,128]{3,2,1,0:T(8,128)(2,1)} %param.10) | copy-start | bytes 2064388
  165.7 77.7 %copy-start.5 = (s32[8]{0:T(128)S(1)}, s32[8]{0:T(128)}, u32[]{:S(2)}) copy-start(s32[8]{0:T(128)} %param.13) | copy-start | bytes 100
  352.7 216.4 %all-reduce.4.cloned.1.call-start = ((), (), s32[]{:S(2)}) async-start(), calls=%async_computation.5 | async-start | bytes 786432 | tf_op jit(solution)/shard_map/psum | solution.py:53
  407.3 14.2 %slice-start = ((s8[6291456]{0:T(1024)(128)(4,1)}), s8[2097152]{0:T(1024)(128)(4,1)S(1)}, s32[]{:S(2)}) async-start(s8[6291456]{0:T(1024)(128)(4,1)} %bitcast.45), calls=%async_computation.7 | async-start | bytes 4194304
  411.3 10.1 %slice-start.1 = ((s8[6291456]{0:T(1024)(128)(4,1)}), s8[4194304]{0:T(1024)(128)(4,1)S(1)}, s32[]{:S(2)}) async-start(s8[6291456]{0:T(1024)(128)(4,1)} %bitcast.45), calls=%async_computation.8 | async-start | bytes 8388608
  424.9 213.4 %all-reduce.6.cloned.1.call-start = ((), (), s32[]{:S(2)}) async-start(), calls=%async_computation.6 | async-start | bytes 1179648 | tf_op jit(solution)/shard_map/psum | solution.py:53
Sparse Core Ops, SparseCore 0:
  24.6 31.9 all-gather.1
  352.8 50.5 reduce-scatter.1
  425.0 144.0 all-reduce.3
  572.0 66.2 all-reduce.5
